TPU v7x, 32 devices: a whole 2x2x4 slice. The times are simulated.
32 devices in a mesh: band: 4 (over z), grid: 8 (over y, x, core).
Axes of the slice: x: 2, y: 2, z: 4, core: 2. Of those that a mesh axis runs over, the one named last changes fastest.
Arguments:
- orbitals: bfloat16 [8, 256, 256, 256], P('band', 'grid'), may hold values from -60 to 60
- potential: float32 [256, 256, 256], P('grid'), may hold values from -2 to 1
Outputs:
- rotated: bfloat16 [8, 256, 256, 256], P('band', 'grid')
- projected: float32 [8, 8], replicated
All inputs are finite; a program needn't handle non-finite values. Where the computation divides by a largest or mean magnitude, that divisor is 1e-20 or more.
Results may differ from a plain program's by a relative error of at most 0.0005.
The roundings to bfloat16 on the way count: a program that leaves them out, or rounds other values in their place, can miss the bound.
Values may be sent and summed in bfloat16 or wider, within the bound.
A program may use at most 192 MiB of HBM per device.

v0:
```python
import math
import jax
import jax.numpy as jnp
from jax import lax
from jax.sharding import PartitionSpec as P

NS_ITERS = 6
CENTER = 9.5
HALF_WIDTH = 6.5


def second_derivative(length):
    index = jnp.arange(length, dtype=jnp.int32)
    product = index[:, None] * index[None, :] % length
    angles = product.astype(jnp.float32) * (2.0 * math.pi / length)
    freq = jnp.minimum(index, length - index).astype(jnp.float32)
    weight = -((2.0 * math.pi / length * freq) ** 2) / length
    cosines = jnp.cos(angles)
    sines = jnp.sin(angles)
    matrix = jnp.dot(cosines * weight[None, :], cosines.T, precision=lax.Precision.HIGHEST)
    matrix = matrix + jnp.dot(sines * weight[None, :], sines.T, precision=lax.Precision.HIGHEST)
    return matrix.astype(jnp.bfloat16)


def apply_ham(field, potential, k_x, k_y, k_z):
    depth = field.shape[3]
    term_z = jnp.dot(field.reshape(-1, depth), k_z, preferred_element_type=jnp.float32).reshape(
        field.shape
    )
    term_y = jnp.einsum("oxjz,jy->oxyz", field, k_y, preferred_element_type=jnp.float32)
    derived = jnp.einsum(
        "ojyz,jx->oxyz",
        lax.all_to_all(field, "grid", split_axis=2, concat_axis=1, tiled=True),
        k_x,
        preferred_element_type=jnp.float32,
    ).astype(jnp.bfloat16)
    term_x = lax.all_to_all(derived, "grid", split_axis=1, concat_axis=2, tiled=True)
    return -0.5 * (term_x.astype(jnp.float32) + term_y + term_z) + potential[None] * field.astype(
        jnp.float32
    )


def ritz(correlation, hamil):
    scale = jnp.max(jnp.sum(jnp.abs(correlation), axis=1))
    current = correlation / scale
    identity = jnp.eye(correlation.shape[0], dtype=jnp.float32)
    inverse_root = identity
    for turn_index in range(NS_ITERS):
        turn = 1.5 * identity - 0.5 * jnp.dot(
            inverse_root, current, precision=lax.Precision.HIGHEST
        )
        current = jnp.dot(current, turn, precision=lax.Precision.HIGHEST)
        inverse_root = jnp.dot(turn, inverse_root, precision=lax.Precision.HIGHEST)
    projected = (
        jnp.dot(
            jnp.dot(inverse_root.T, hamil, precision=lax.Precision.HIGHEST),
            inverse_root,
            precision=lax.Precision.HIGHEST,
        )
        / scale
    )
    return (inverse_root.astype(jnp.bfloat16), projected)


def inner_rows(left, right):
    return lax.dot_general(
        left, right, (((1,), (1,)), ((), ())), preferred_element_type=jnp.float32
    )


def per_device(orbitals, potential):
    own = orbitals.shape[0]
    k_x = second_derivative(orbitals.shape[1] * lax.axis_size("grid"))
    k_y = second_derivative(orbitals.shape[2])
    k_z = second_derivative(orbitals.shape[3])
    start_f = orbitals.astype(jnp.float32)
    first = (
        (apply_ham(orbitals, potential, k_x, k_y, k_z) - CENTER * start_f) / HALF_WIDTH
    ).astype(jnp.bfloat16)
    first_f = first.astype(jnp.float32)
    filtered = (
        2.0 * (apply_ham(first, potential, k_x, k_y, k_z) - CENTER * first_f) / HALF_WIDTH - start_f
    ).astype(jnp.bfloat16)
    applied = apply_ham(filtered, potential, k_x, k_y, k_z).astype(jnp.bfloat16)
    gathered = lax.all_gather(filtered, "band", axis=0, tiled=True)
    total = gathered.shape[0]
    flat = gathered.reshape(total, -1)
    s_rows = inner_rows(filtered.reshape(own, -1), flat)
    h_rows = inner_rows(applied.reshape(own, -1), flat)
    s_rows, h_rows = lax.psum((s_rows, h_rows), "grid")
    correlation, hamil = (
        lax.all_gather(s_rows, "band", axis=0, tiled=True),
        lax.all_gather(h_rows, "band", axis=0, tiled=True),
    )
    coeff, projected = ritz(correlation, hamil)
    columns = lax.dynamic_slice_in_dim(coeff, lax.axis_index("band") * own, own, 1)
    mine = lax.dot_general(
        columns, flat, (((0,), (0,)), ((), ())), preferred_element_type=jnp.float32
    )
    rotated = mine.astype(jnp.bfloat16).reshape(filtered.shape)
    return (rotated, projected)


def solution(mesh):
    in_specs = (P("band", "grid", None, None), P("grid", None, None))
    out_specs = (P("band", "grid", None, None), P())
    return jax.shard_map(
        per_device, mesh=mesh, in_specs=in_specs, out_specs=out_specs, check_vma=False
    )
```

profile of v0, /device:TPU:0, one launch (start us, length us, event | category | flops | bytes accessed | tf_op | source)
XLA Modules:
  0.0 1303.1 jit_solution(14852924869631262509)
XLA Ops:
  7.2 11.6 copy.65
  26.9 91.7 %all-to-all-done = bf16[2,32,256,256]{3,1,0,2:T(8,128)(2,1)} async-done(((bf16[2,32,256,256]{3,1,0,2:T(8,128)(2,1)}), bf16[2,32,256,256]{3,1,0,2:T(8,128)(2,1)}, u32[]{:S(2)}, u32[]{:S(2)}) %all-to-all-start) | async-done | bytes 8388640 | tf_op jit(solution)/shard_map/all_to_all | solution.py:33
  126.8 9.0 convert_bitcast_fusion.2
  135.8 11.5 copy.68
  152.5 11.5 convolution_bitcast_fusion
  164.0 17.5 %copy.71 = f32[16384,256]{1,0:T(8,128)} copy(f32[16384,256]{0,1:T(8,128)} %convolution_bitcast_fusion) | data formatting | bytes 33554432 | tf_op jit(solution)/shard_map/dot_general | solution.py:27
  181.5 65.1 %all-to-all-done.1 = bf16[2,256,32,256]{3,2,0,1:T(8,128)(2,1)} async-done(((bf16[2,256,32,256]{3,2,0,1:T(8,128)(2,1)}), bf16[2,256,32,256]{3,2,0,1:T(8,128)(2,1)}, u32[]{:S(2)}, u32[]{:S(2)}) %all-to-all-start.1) | async-done | bytes 8388640 | tf_op jit(solution)/shard_map/all_to_all | solution.py:37
  246.6 11.3 copy.69
  257.9 23.2 %fusion.10 = bf16[2,32,256,256]{3,2,1,0:T(8,128)(2,1)} fusion(bf16[2,32,256,256]{3,2,1,0:T(8,128)(2,1)} %param.2, f32[2,32,256,256]{3,2,1,0:T(8,128)} %bitcast.160, f32[2,8,32,32,256]{4,3,1,2,0:T(8,128)} %copy.69, f32[32,256,256]{2,1,0:T(8,128)} %param.3, bf16[256,256]{1,0:T(8,128)(2,1)S(1)} %fusion.22), kind=kOutput, calls=%fused_computation.17 | convolution fusion | flops 2189426688 | bytes 58851328 | tf_op jit(solution)/shard_map/oxjz,jy->oxyz/dot_general | solution.py:30
  281.1 11.4 copy.72
  292.5 100.1 %all_to_all.81 = bf16[2,32,256,256]{3,1,0,2:T(8,128)(2,1)} all-to-all(bf16[2,32,256,256]{3,1,0,2:T(8,128)(2,1)} %copy.72), channel_id=1, replica_groups=mesh['band'=4,'grid'=8] {'grid'}, dimensions={2} | all-to-all | bytes 16777216 | tf_op jit(solution)/shard_map/all_to_all | solution.py:33
  400.6 9.0 convert_bitcast_fusion.1
  409.6 11.4 copy.75
  426.2 11.5 fusion.55
  437.6 82.3 %all-to-all-done.3 = bf16[2,256,32,256]{3,2,0,1:T(8,128)(2,1)} async-done(((bf16[2,256,32,256]{3,2,0,1:T(8,128)(2,1)}), bf16[2,256,32,256]{3,2,0,1:T(8,128)(2,1)}, u32[]{:S(2)}, u32[]{:S(2)}) %all-to-all-start.3) | async-done | bytes 8388640 | tf_op jit(solution)/shard_map/all_to_all | solution.py:37
  520.0 11.3 copy.76
  531.3 26.1 %fusion.11 = bf16[2,32,256,256]{3,2,1,0:T(8,128)(2,1)} fusion(bf16[2,32,256,256]{3,2,1,0:T(8,128)(2,1)} %param.2, bf16[2,32,256,256]{3,2,1,0:T(8,128)(2,1)} %fusion.10, f32[2,8,32,32,256]{4,3,1,2,0:T(8,128)} %copy.76, f32[256,2,32,256]{3,0,2,1:T(8,128)} %fusion.55, f32[32,256,256]{2,1,0:T(8,128)} %param.3, bf16[256,256]{1,0:T(8,128)(2,1)S(1)} %fusion.22), kind=kOutput, calls=%fused_computation.18 | convolution fusion | flops 2197815296 | bytes 67239936 | tf_op jit(solution)/shard_map/dot_general | solution.py:27
  557.4 13.7 %copy.81 = bf16[2,32,256,256]{3,1,0,2:T(8,128)(2,1)} copy(bf16[2,32,256,256]{3,2,1,0:T(8,128)(2,1)} %fusion.11) | data formatting | bytes 16777216 | tf_op jit(solution)/shard_map/convert_element_type | solution.py:83
  571.1 100.2 %all_to_all.82 = bf16[2,32,256,256]{3,1,0,2:T(8,128)(2,1)} all-to-all(bf16[2,32,256,256]{3,1,0,2:T(8,128)(2,1)} %copy.81), channel_id=1, replica_groups=mesh['band'=4,'grid'=8] {'grid'}, dimensions={2} | all-to-all | bytes 16777216 | tf_op jit(solution)/shard_map/all_to_all | solution.py:33
  679.6 9.0 convert_bitcast_fusion
  688.6 11.6 copy.84
  705.2 11.5 fusion.50
  716.6 82.6 %all-to-all-done.5 = bf16[2,256,32,256]{3,2,0,1:T(8,128)(2,1)} async-done(((bf16[2,256,32,256]{3,2,0,1:T(8,128)(2,1)}), bf16[2,256,32,256]{3,2,0,1:T(8,128)(2,1)}, u32[]{:S(2)}, u32[]{:S(2)}) %all-to-all-start.5) | async-done | bytes 8388640 | tf_op jit(solution)/shard_map/all_to_all | solution.py:37
  799.2 11.3 copy.85
  810.5 23.3 %fusion.15 = bf16[2,32,256,256]{3,2,1,0:T(8,128)(2,1)} fusion(f32[2,8,32,32,256]{4,3,1,2,0:T(8,128)} %copy.85, f32[256,2,32,256]{3,0,2,1:T(8,128)} %fusion.50, bf16[2,32,256,256]{3,2,1,0:T(8,128)(2,1)} %fusion.11, f32[32,256,256]{2,1,0:T(8,128)} %param.3, bf16[256,256]{1,0:T(8,128)(2,1)S(1)} %fusion.22), kind=kOutput, calls=%fused_computation.23 | convolution fusion | flops 2176843776 | bytes 58851328 | tf_op jit(solution)/shard_map/dot_general | solution.py:27
  833.8 285.2 %all-gather.4.cloned.1.call-done = bf16[8,32,256,256]{3,2,1,0:T(8,128)(2,1)} async-done(((bf16[2,32,256,256]{3,2,1,0:T(8,128)(2,1)}), bf16[8,32,256,256]{3,2,1,0:T(8,128)(2,1)}) %all-gather.4.cloned.1.call-update) | async-done | bytes 33554448 | tf_op jit(solution)/shard_map/all_gather | solution.py:85
  1119.0 49.8 %fusion.29 = f32[2,8]{1,0:T(2,128)S(1)} fusion(bf16[8,32,256,256]{3,2,1,0:T(8,128)(2,1)} %all-gather.4.cloned.1.call-done, bf16[2,32,256,256]{3,2,1,0:T(8,128)(2,1)} %fusion.11), kind=kOutput, calls=%fused_computation.50 | convolution fusion | flops 67108864 | bytes 41943104 | tf_op jit(solution)/shard_map/dot_general | solution.py:66
  1168.8 34.6 %fusion.34 = f32[2,8]{1,0:T(2,128)S(1)} fusion(bf16[8,32,256,256]{3,2,1,0:T(8,128)(2,1)} %all-gather.4.cloned.1.call-done, bf16[2,32,256,256]{3,2,1,0:T(8,128)(2,1)S(1)} %copy-done), kind=kOutput, calls=%fused_computation.51 | convolution fusion | flops 67108864 | bytes 41943104 | tf_op jit(solution)/shard_map/dot_general | solution.py:66
  1203.4 13.8 %all-reduce = (f32[2,8]{1,0:T(2,128)S(1)}, f32[2,8]{1,0:T(2,128)S(1)}) all-reduce(f32[2,8]{1,0:T(2,128)S(1)} %fusion.29, f32[2,8]{1,0:T(2,128)S(1)} %fusion.34), channel_id=1, replica_groups=mesh['band'=4,'grid'=8] {'grid'}, use_global_device_ids=true, to_apply=%region_0.1 | all-reduce | flops 32 | bytes 256 | tf_op jit(solution)/shard_map/psum | solution.py:90
  1228.9 9.1 all-gather.1
  1239.5 31.1 %copy.105 = bf16[1,8,8192,256]{3,1,2,0:T(8,128)(2,1)} copy(bf16[1,8,8192,256]{3,2,1,0:T(8,128)(2,1)} %bitcast.162) | data formatting | bytes 67108864
  1270.6 17.5 %convolution_convert_fusion = bf16[2,2097152]{1,0:T(2,128)(2,1)} fusion(bf16[8,2097152]{1,0:T(8,128)(2,1)} %bitcast.158, bf16[8,8]{0,1:T(8,128)(2,1)S(1)} %get-tuple-element.4, s32[]{:T(128)S(6)} %select_n.21), kind=kOutput, calls=%fused_computation | convolution fusion | flops 71303168 | bytes 41943556 | tf_op jit(solution)/shard_map/dot_general | solution.py:97
  (38 shorter events, 69.2 us)
Async XLA Ops:
  18.7 99.9 %all-to-all-start = ((bf16[2,32,256,256]{3,1,0,2:T(8,128)(2,1)}), bf16[2,32,256,256]{3,1,0,2:T(8,128)(2,1)}, u32[]{:S(2)}, u32[]{:S(2)}) async-start(bf16[2,32,256,256]{3,1,0,2:T(8,128)(2,1)} %copy.65), calls=%async_computation | async-start | bytes 16777216 | tf_op jit(solution)/shard_map/all_to_all | solution.py:33
  147.4 99.2 %all-to-all-start.1 = ((bf16[2,256,32,256]{3,2,0,1:T(8,128)(2,1)}), bf16[2,256,32,256]{3,2,0,1:T(8,128)(2,1)}, u32[]{:S(2)}, u32[]{:S(2)}) async-start(bf16[2,256,32,256]{3,2,0,1:T(8,128)(2,1)} %copy.68), calls=%async_computation.1 | async-start | bytes 16777216 | tf_op jit(solution)/shard_map/all_to_all | solution.py:37
  421.0 99.0 %all-to-all-start.3 = ((bf16[2,256,32,256]{3,2,0,1:T(8,128)(2,1)}), bf16[2,256,32,256]{3,2,0,1:T(8,128)(2,1)}, u32[]{:S(2)}, u32[]{:S(2)}) async-start(bf16[2,256,32,256]{3,2,0,1:T(8,128)(2,1)} %copy.75), calls=%async_computation.3 | async-start | bytes 16777216 | tf_op jit(solution)/shard_map/all_to_all | solution.py:37
  425.9 693.1 %all-gather.4.cloned.1.call-start = ((), (), s32[]{:S(2)}) async-start(), calls=%async_computation.6 | async-start | bytes 41943040 | tf_op jit(solution)/shard_map/all_gather | solution.py:85
  700.2 99.0 %all-to-all-start.5 = ((bf16[2,256,32,256]{3,2,0,1:T(8,128)(2,1)}), bf16[2,256,32,256]{3,2,0,1:T(8,128)(2,1)}, u32[]{:S(2)}, u32[]{:S(2)}) async-start(bf16[2,256,32,256]{3,2,0,1:T(8,128)(2,1)} %copy.84), calls=%async_computation.5 | async-start | bytes 16777216 | tf_op jit(solution)/shard_map/all_to_all | solution.py:37
  1119.0 49.8 %copy-start = (bf16[2,32,256,256]{3,2,1,0:T(8,128)(2,1)S(1)}, bf16[2,32,256,256]{3,2,1,0:T(8,128)(2,1)}, u32[]{:S(2)}) copy-start(bf16[2,32,256,256]{3,2,1,0:T(8,128)(2,1)} %fusion.15) | copy-start | bytes 25165828
Sparse Core Ops, SparseCore 0:
  557.5 561.5 all-gather.3
where the time goes:
time: 1310 us; the launch traced here: 1300 us
  waiting for transfers between devices  607 us (46%)
  matrix products  242 us (18%)
  blocking collectives  231 us (18%)
  local copies, waits for them, and re-layouts  186 us (14%)
  starting transfers between devices  20.7 us (2%)
  between operations  14.3 us (1%)
    all_gather x1, waiting for transfers between devices, per_device(): gathered = lax.all_gather(filtered, 'band', axis=0, tiled=True)  285 us
    all_to_all x3, waiting for transfers between devices, apply_ham(): lax.all_to_all(derived, 'grid', split_axis=1, concat_axis=2, tiled=True)  230 us
    all_to_all x2, blocking collectives, apply_ham(): lax.all_to_all(field, 'grid', split_axis=2, concat_axis=1, tiled=True)  200 us
    all_to_all x1, waiting for transfers between devices, apply_ham(): lax.all_to_all(field, 'grid', split_axis=2, concat_axis=1, tiled=True)  91.7 us
    dot_general x2, matrix products, inner_rows(): lax.dot_general(left, right, (((1,), (1,)), ((), ())), preferred_element_...  84.3 us
    dot_general x3, matrix products, apply_ham(): jnp.dot(field.reshape(-1, depth), k_z, preferred_element_type=jnp.float32)  60.8 us
    unnamed x5, local copies, waits for them, and re-layouts  50.5 us
    dot_general x3, matrix products, apply_ham(): jnp.einsum('oxjz,jy->oxyz', field, k_y, preferred_element_type=jnp.float32)  46.2 us
  transfers between devices with their start and end apart: 5, of which 5 were waited for; matrix products, arithmetic and copies ran while one was open for 10% of the time, Pallas kernels for 0%

commit v1 on v0

--- a/solution.py
+++ b/solution.py
@@ -82,7 +82,14 @@
         2.0 * (apply_ham(first, potential, k_x, k_y, k_z) - CENTER * first_f) / HALF_WIDTH - start_f
     ).astype(jnp.bfloat16)
     applied = apply_ham(filtered, potential, k_x, k_y, k_z).astype(jnp.bfloat16)
-    gathered = lax.all_gather(filtered, "band", axis=0, tiled=True)
+    devices = lax.axis_size("band")
+    route = [(i, (i + 1) % devices) for i in range(devices)]
+    parts = [filtered]
+    for hop in range(1, devices):
+        parts = [lax.ppermute(parts[0], "band", route), *parts]
+    full = jnp.concatenate(parts, axis=0)
+    turn_2 = (lax.axis_index("band") + 1) * parts[-1].shape[0]
+    gathered = jnp.roll(full, turn_2, axis=0)
     total = gathered.shape[0]
     flat = gathered.reshape(total, -1)
     s_rows = inner_rows(filtered.reshape(own, -1), flat)

time: 1310 us -> 1380 us (1.053)
  blocking collectives: 231 us -> 136 us
  local copies, waits for them, and re-layouts: 186 us -> 268 us
  waiting for transfers between devices: 607 us -> 684 us
  matrix products: 242 us -> 257 us
    ppermute x0 -> x3, waiting for transfers between devices: none -> 444 us  [per_device(): parts = [lax.ppermute(parts[0], 'band', route), *parts]]
    all_gather x1 -> x0, waiting for transfers between devices: 285 us -> none  [per_device(): gathered = lax.all_gather(filtered, 'band', axis=0, tiled=True)]
    all_to_all x2 -> x1, blocking collectives: 200 us -> 99.9 us  [apply_ham(): lax.all_to_all(field, 'grid', split_axis=2, concat_axis=1, tiled=True)]
    all_to_all x3, waiting for transfers between devices: 230 us -> 148 us  [apply_ham(): lax.all_to_all(derived, 'grid', split_axis=1, concat_axis=2, tiled=True)]
    unnamed x5 -> x10, local copies, waits for them, and re-layouts: 50.5 us -> 104 us
    dynamic_slice x0 -> x1, local copies, waits for them, and re-layouts: none -> 23 us  [per_device(): gathered = jnp.roll(full, turn_2, axis=0)]
    dot_general x2, matrix products: 84.3 us -> 99.6 us  [inner_rows(): lax.dot_general(left, right, (((1,), (1,)), ((), ())), preferred_element_...]
    all_to_all x1 -> x2, waiting for transfers between devices: 91.7 us -> 91.7 us  [apply_ham(): lax.all_to_all(field, 'grid', split_axis=2, concat_axis=1, tiled=True)]
  transfers between devices with their start and end apart: 5 -> 8, of which waited for: 5 -> 6; matrix products, arithmetic and copies ran while one was open for 10% -> 9% of each run, Pallas kernels for 0% -> 0%
where the time goes in v1:
time: 1380 us
  waiting for transfers between devices  684 us (50%)
  local copies, waits for them, and re-layouts  268 us (19%)
  matrix products  257 us (19%)
  blocking collectives  136 us (10%)
  starting transfers between devices  29 us (2%)
    ppermute x3, waiting for transfers between devices, per_device(): parts = [lax.ppermute(parts[0], 'band', route), *parts]  444 us
    all_to_all x3, waiting for transfers between devices, apply_ham(): lax.all_to_all(derived, 'grid', split_axis=1, concat_axis=2, tiled=True)  148 us
    unnamed x10, local copies, waits for them, and re-layouts  104 us
    all_to_all x1, blocking collectives, apply_ham(): lax.all_to_all(field, 'grid', split_axis=2, concat_axis=1, tiled=True)  99.9 us
    dot_general x2, matrix products, inner_rows(): lax.dot_general(left, right, (((1,), (1,)), ((), ())), preferred_element_...  99.6 us
    all_to_all x2, waiting for transfers between devices, apply_ham(): lax.all_to_all(field, 'grid', split_axis=2, concat_axis=1, tiled=True)  91.7 us
    dot_general x3, matrix products, apply_ham(): jnp.dot(field.reshape(-1, depth), k_z, preferred_element_type=jnp.float32)  60.6 us
    dot_general x3, matrix products, apply_ham(): jnp.einsum('oxjz,jy->oxyz', field, k_y, preferred_element_type=jnp.float32)  46.2 us
  transfers between devices with their start and end apart: 8, of which 6 were waited for; matrix products, arithmetic and copies ran while one was open for 9% of the time, Pallas kernels for 0%

profile of v1, /device:TPU:0, one launch (start us, length us, event | category | flops | bytes accessed | tf_op | source)
XLA Modules:
  0.0 1376.2 jit_solution(7244123992208639853)
XLA Ops:
  0.6 11.6 copy.65
  20.5 91.7 %all-to-all-done = bf16[2,32,256,256]{3,1,0,2:T(8,128)(2,1)} async-done(((bf16[2,32,256,256]{3,1,0,2:T(8,128)(2,1)}), bf16[2,32,256,256]{3,1,0,2:T(8,128)(2,1)}, u32[]{:S(2)}, u32[]{:S(2)}) %all-to-all-start) | async-done | bytes 8388640 | tf_op jit(solution)/shard_map/all_to_all | solution.py:33
  120.4 9.0 convert_bitcast_fusion.2
  129.4 11.5 copy.68
  146.4 11.5 convolution_bitcast_fusion
  158.0 17.4 %copy.71 = f32[16384,256]{1,0:T(8,128)} copy(f32[16384,256]{0,1:T(8,128)} %convolution_bitcast_fusion) | data formatting | bytes 33554432 | tf_op jit(solution)/shard_map/dot_general | solution.py:27
  175.4 65.1 %all-to-all-done.1 = bf16[2,256,32,256]{3,2,0,1:T(8,128)(2,1)} async-done(((bf16[2,256,32,256]{3,2,0,1:T(8,128)(2,1)}), bf16[2,256,32,256]{3,2,0,1:T(8,128)(2,1)}, u32[]{:S(2)}, u32[]{:S(2)}) %all-to-all-start.1) | async-done | bytes 8388640 | tf_op jit(solution)/shard_map/all_to_all | solution.py:37
  240.5 11.3 copy.69
  251.8 23.3 %fusion.10 = bf16[2,32,256,256]{3,2,1,0:T(8,128)(2,1)} fusion(bf16[2,32,256,256]{3,2,1,0:T(8,128)(2,1)} %param.2, f32[2,32,256,256]{3,2,1,0:T(8,128)} %bitcast.161, f32[2,8,32,32,256]{4,3,1,2,0:T(8,128)} %copy.69, f32[32,256,256]{2,1,0:T(8,128)} %param.3, bf16[256,256]{1,0:T(8,128)(2,1)S(1)} %fusion.22), kind=kOutput, calls=%fused_computation.17 | convolution fusion | flops 2189426688 | bytes 58851328 | tf_op jit(solution)/shard_map/oxjz,jy->oxyz/dot_general | solution.py:30
  275.1 11.4 copy.72
  286.4 99.9 %all_to_all.81 = bf16[2,32,256,256]{3,1,0,2:T(8,128)(2,1)} all-to-all(bf16[2,32,256,256]{3,1,0,2:T(8,128)(2,1)} %copy.72), channel_id=1, replica_groups=mesh['band'=4,'grid'=8] {'grid'}, dimensions={2} | all-to-all | bytes 16777216 | tf_op jit(solution)/shard_map/all_to_all | solution.py:33
  403.4 11.4 copy.75
  419.9 11.5 fusion.55
  431.4 82.6 %all-to-all-done.3 = bf16[2,256,32,256]{3,2,0,1:T(8,128)(2,1)} async-done(((bf16[2,256,32,256]{3,2,0,1:T(8,128)(2,1)}), bf16[2,256,32,256]{3,2,0,1:T(8,128)(2,1)}, u32[]{:S(2)}, u32[]{:S(2)}) %all-to-all-start.3) | async-done | bytes 8388640 | tf_op jit(solution)/shard_map/all_to_all | solution.py:37
  513.9 11.3 copy.76
  525.3 26.1 %fusion.11 = bf16[2,32,256,256]{3,2,1,0:T(8,128)(2,1)} fusion(bf16[2,32,256,256]{3,2,1,0:T(8,128)(2,1)} %param.2, bf16[2,32,256,256]{3,2,1,0:T(8,128)(2,1)} %fusion.10, f32[2,8,32,32,256]{4,3,1,2,0:T(8,128)} %copy.76, f32[256,2,32,256]{3,0,2,1:T(8,128)} %fusion.55, f32[32,256,256]{2,1,0:T(8,128)} %param.3, bf16[256,256]{1,0:T(8,128)(2,1)S(1)} %fusion.22), kind=kOutput, calls=%fused_computation.18 | convolution fusion | flops 2197815296 | bytes 67239936 | tf_op jit(solution)/shard_map/dot_general | solution.py:27
  553.6 11.6 copy.81
  570.2 163.3 %collective-permute-done = bf16[2,32,256,256]{3,2,1,0:T(8,128)(2,1)} collective-permute-done((bf16[2,32,256,256]{3,2,1,0:T(8,128)(2,1)}, bf16[2,32,256,256]{3,2,1,0:T(8,128)(2,1)}, u32[]{:S(2)}, u32[]{:S(2)}) %collective-permute-start) | collective-permute-done | bytes 8388640 | tf_op jit(solution)/shard_map/ppermute | solution.py:89
  742.2 9.0 convert_bitcast_fusion
  751.2 11.5 copy.84
  767.7 147.0 %collective-permute-done.1 = bf16[2,32,256,256]{3,2,1,0:T(8,128)(2,1)} collective-permute-done((bf16[2,32,256,256]{3,2,1,0:T(8,128)(2,1)}, bf16[2,32,256,256]{3,2,1,0:T(8,128)(2,1)}, u32[]{:S(2)}, u32[]{:S(2)}) %collective-permute-start.1) | collective-permute-done | bytes 8388640 | tf_op jit(solution)/shard_map/ppermute | solution.py:89
  914.9 11.5 fusion.50
  926.4 11.3 copy.85
  937.7 23.0 %fusion.15 = bf16[2,32,256,256]{3,2,1,0:T(8,128)(2,1)} fusion(f32[2,8,32,32,256]{4,3,1,2,0:T(8,128)} %copy.85, f32[256,2,32,256]{3,0,2,1:T(8,128)} %fusion.50, bf16[2,32,256,256]{3,2,1,0:T(8,128)(2,1)} %fusion.11, f32[32,256,256]{2,1,0:T(8,128)} %param.3, bf16[256,256]{1,0:T(8,128)(2,1)S(1)} %fusion.22), kind=kOutput, calls=%fused_computation.23 | convolution fusion | flops 2176843776 | bytes 58851328 | tf_op jit(solution)/shard_map/dot_general | solution.py:27
  960.7 134.1 %collective-permute-done.2 = bf16[2,32,256,256]{3,2,1,0:T(8,128)(2,1)} collective-permute-done((bf16[2,32,256,256]{3,2,1,0:T(8,128)(2,1)}, bf16[2,32,256,256]{3,2,1,0:T(8,128)(2,1)}, u32[]{:S(2)}, u32[]{:S(2)}) %collective-permute-start.2) | collective-permute-done | bytes 8388640 | tf_op jit(solution)/shard_map/ppermute | solution.py:89
  1155.6 23.0 %constant_dynamic-slice_fusion = bf16[8,32,256,256]{3,2,1,0:T(8,128)(2,1)} fusion(bf16[16,32,256,256]{3,2,1,0:T(8,128)(2,1)} %constant_dynamic-update-slice_fusion, s32[]{:T(128)S(6)} %select_n.34), kind=kLoop, calls=%fused_computation.99 | loop fusion | bytes 67108864 | tf_op jit(solution)/shard_map/jit(_roll_dynamic)/dynamic_slice | solution.py:92
  1178.6 49.7 %fusion.29 = f32[2,8]{1,0:T(2,128)S(1)} fusion(bf16[8,32,256,256]{3,2,1,0:T(8,128)(2,1)} %constant_dynamic-slice_fusion, bf16[2,32,256,256]{3,2,1,0:T(8,128)(2,1)} %fusion.11), kind=kOutput, calls=%fused_computation.50 | convolution fusion | flops 67108864 | bytes 41943104 | tf_op jit(solution)/shard_map/dot_general | solution.py:66
  1228.3 49.9 %fusion.34 = f32[2,8]{1,0:T(2,128)S(1)} fusion(bf16[8,32,256,256]{3,2,1,0:T(8,128)(2,1)} %constant_dynamic-slice_fusion, bf16[2,32,256,256]{3,2,1,0:T(8,128)(2,1)} %fusion.15), kind=kOutput, calls=%fused_computation.51 | convolution fusion | flops 67108864 | bytes 41943104 | tf_op jit(solution)/shard_map/dot_general | solution.py:66
  1278.1 18.8 %all-reduce = (f32[2,8]{1,0:T(2,128)S(1)}, f32[2,8]{1,0:T(2,128)S(1)}) all-reduce(f32[2,8]{1,0:T(2,128)S(1)} %fusion.29, f32[2,8]{1,0:T(2,128)S(1)} %fusion.34), channel_id=1, replica_groups=mesh['band'=4,'grid'=8] {'grid'}, use_global_device_ids=true, to_apply=%region_0.1 | all-reduce | flops 32 | bytes 256 | tf_op jit(solution)/shard_map/psum | solution.py:97
  1308.3 9.6 all-gather.1
  1319.4 31.2 %copy.105 = bf16[1,8,8192,256]{3,1,2,0:T(8,128)(2,1)} copy(bf16[1,8,8192,256]{3,2,1,0:T(8,128)(2,1)} %bitcast.159) | data formatting | bytes 67108864
  1350.6 17.5 %convolution_convert_fusion = bf16[2,2097152]{1,0:T(2,128)(2,1)} fusion(bf16[8,2097152]{1,0:T(8,128)(2,1)} %bitcast.158, bf16[8,8]{0,1:T(8,128)(2,1)S(1)} %get-tuple-element.4, s32[]{:T(128)S(6)} %select_n.35), kind=kOutput, calls=%fused_computation | convolution fusion | flops 71303168 | bytes 41943556 | tf_op jit(solution)/shard_map/dot_general | solution.py:104
  (49 shorter events, 146.7 us)
Async XLA Ops:
  12.2 100.0 %all-to-all-start = ((bf16[2,32,256,256]{3,1,0,2:T(8,128)(2,1)}), bf16[2,32,256,256]{3,1,0,2:T(8,128)(2,1)}, u32[]{:S(2)}, u32[]{:S(2)}) async-start(bf16[2,32,256,256]{3,1,0,2:T(8,128)(2,1)} %copy.65), calls=%async_computation | async-start | bytes 16777216 | tf_op jit(solution)/shard_map/all_to_all | solution.py:33
  141.0 99.5 %all-to-all-start.1 = ((bf16[2,256,32,256]{3,2,0,1:T(8,128)(2,1)}), bf16[2,256,32,256]{3,2,0,1:T(8,128)(2,1)}, u32[]{:S(2)}, u32[]{:S(2)}) async-start(bf16[2,256,32,256]{3,2,0,1:T(8,128)(2,1)} %copy.68), calls=%async_computation.1 | async-start | bytes 16777216 | tf_op jit(solution)/shard_map/all_to_all | solution.py:37
  414.7 99.2 %all-to-all-start.3 = ((bf16[2,256,32,256]{3,2,0,1:T(8,128)(2,1)}), bf16[2,256,32,256]{3,2,0,1:T(8,128)(2,1)}, u32[]{:S(2)}, u32[]{:S(2)}) async-start(bf16[2,256,32,256]{3,2,0,1:T(8,128)(2,1)} %copy.75), calls=%async_computation.3 | async-start | bytes 16777216 | tf_op jit(solution)/shard_map/all_to_all | solution.py:37
  551.3 182.2 %collective-permute-start = (bf16[2,32,256,256]{3,2,1,0:T(8,128)(2,1)}, bf16[2,32,256,256]{3,2,1,0:T(8,128)(2,1)}, u32[]{:S(2)}, u32[]{:S(2)}) collective-permute-start(bf16[2,32,256,256]{3,2,1,0:T(8,128)(2,1)} %fusion.11), channel_id=1, source_target_pairs={{0,8},{8,16},{16,24},{24,0},{1,9},{9,17},{17,25},{25,1},{2,10},{10... | collective-permute-start | bytes 25165832 | tf_op jit(solution)/shard_map/ppermute | solution.py:89
  565.2 168.7 %all-to-all-start.4 = ((bf16[2,32,256,256]{3,1,0,2:T(8,128)(2,1)}), bf16[2,32,256,256]{3,1,0,2:T(8,128)(2,1)}, u32[]{:S(2)}, u32[]{:S(2)}) async-start(bf16[2,32,256,256]{3,1,0,2:T(8,128)(2,1)} %copy.81), calls=%async_computation.4 | async-start | bytes 16777216 | tf_op jit(solution)/shard_map/all_to_all | solution.py:33
  733.5 181.2 %collective-permute-start.1 = (bf16[2,32,256,256]{3,2,1,0:T(8,128)(2,1)}, bf16[2,32,256,256]{3,2,1,0:T(8,128)(2,1)}, u32[]{:S(2)}, u32[]{:S(2)}) collective-permute-start(bf16[2,32,256,256]{3,2,1,0:T(8,128)(2,1)} %collective-permute-done), channel_id=1, source_target_pairs={{0,8},{8,16},{16,24},{24,0},{1,9},{9,17},{17,25},{25,1},{2,10},{10... | collective-permute-start | bytes 25165832 | tf_op jit(solution)/shard_map/ppermute | solution.py:89
  762.7 163.7 %all-to-all-start.5 = ((bf16[2,256,32,256]{3,2,0,1:T(8,128)(2,1)}), bf16[2,256,32,256]{3,2,0,1:T(8,128)(2,1)}, u32[]{:S(2)}, u32[]{:S(2)}) async-start(bf16[2,256,32,256]{3,2,0,1:T(8,128)(2,1)} %copy.84), calls=%async_computation.5 | async-start | bytes 16777216 | tf_op jit(solution)/shard_map/all_to_all | solution.py:37
  914.8 180.1 %collective-permute-start.2 = (bf16[2,32,256,256]{3,2,1,0:T(8,128)(2,1)}, bf16[2,32,256,256]{3,2,1,0:T(8,128)(2,1)}, u32[]{:S(2)}, u32[]{:S(2)}) collective-permute-start(bf16[2,32,256,256]{3,2,1,0:T(8,128)(2,1)} %collective-permute-done.1), channel_id=1, source_target_pairs={{0,8},{8,16},{16,24},{24,0},{1,9},{9,17},{17,25},{25,1},{2,10},{10... | collective-permute-start | bytes 25165832 | tf_op jit(solution)/shard_map/ppermute | solution.py:89
